TPU v7x, 128 devices: a whole 4x4x4 slice. The times are simulated.
128 devices in a mesh: row: 16 (over z_hi, y, core), col: 8 (over z_lo, x).
Axes of the slice: x: 4, y: 4, z: 4 (z_hi: 2, z_lo: 2; z = z_hi * 2 + z_lo), core: 2. Of those that a mesh axis runs over, the one named last changes fastest.
Arguments:
- grad_out: bfloat16 [262144, 256], P(('row', 'col')), may hold values from -6 to 6
- preact: bfloat16 [262144, 256], P(('row', 'col')), may hold values from -6 to 6
- features: bfloat16 [262144, 256], P(('col', 'row')), may hold values from -6 to 6
- weight: bfloat16 [256, 256], replicated, may hold values from -0.375 to 0.375
- tiles: bfloat16 [16, 8, 320, 128, 128], P('row', 'col'), may hold values from -0.099609375 to 0.099609375
- tile_rows: int32 [16, 8, 320], P('row', 'col'), may hold values from 0 to 127
- tile_cols: int32 [16, 8, 320], P('row', 'col'), may hold values from 0 to 255
- live_counts: int32 [16, 8], P('row', 'col'), may hold values from 80 to 320, as said below
Outputs:
- grad_features: bfloat16 [262144, 256], P(('col', 'row'))
- grad_weight: float32 [256, 256], replicated
Inputs may be any that keep to these rules, and one draw needn't show every extreme that they name: `live_counts`: some block holds exactly 320 live tiles in every draw.
All inputs are finite; a program needn't handle non-finite values.
Results may differ from a plain program's by a relative error of at most 0.02.
Values may be sent and summed in bfloat16 or wider, within the bound.
A program may use at most 192 MiB of HBM per device.

v0:
```python
import math
import jax
import jax.numpy as jnp
from jax import lax
from jax.sharding import PartitionSpec as P


def body(grad_out, preact, features, weight, tiles, tile_rows, tile_cols, live_counts):
    width = grad_out.shape[1]
    masked = jnp.where(preact > 0, grad_out, jnp.zeros_like(grad_out))
    block = lax.all_gather(masked, "col", axis=0, tiled=True)
    row_count = block.shape[0] // 128
    row_flat = block.reshape(row_count, 128 * width)
    slots = tiles.shape[2]
    tile_stack = tiles.reshape(slots, 128, 128)
    row_index = tile_rows.reshape(slots)
    col_index = tile_cols.reshape(slots)
    count = live_counts.reshape(())
    col_tiles = lax.axis_size("row") * grad_out.shape[0] // 128
    group = math.gcd(slots, 32)
    offsets = jnp.arange(group, dtype=jnp.int32)
    row_ids = jnp.arange(row_count, dtype=jnp.int32)
    col_ids = jnp.arange(col_tiles, dtype=jnp.int32)

    def add_group(step, accum):
        start = step * group
        tile_blk = lax.dynamic_slice_in_dim(tile_stack, start, group, 0)
        rows_now = lax.dynamic_slice_in_dim(row_index, start, group, 0)
        cols_now = lax.dynamic_slice_in_dim(col_index, start, group, 0) - 0
        pick = (rows_now[:, None] == row_ids[None, :]).astype(jnp.bfloat16)
        gathered = jnp.dot(pick, row_flat, preferred_element_type=jnp.float32).astype(jnp.bfloat16)
        gathered = gathered.reshape(group, 128, width)
        prod = jnp.einsum("kab,kaf->kbf", tile_blk, gathered, preferred_element_type=jnp.float32)
        upper = prod.astype(jnp.bfloat16)
        lower = (prod - upper.astype(jnp.float32)).astype(jnp.bfloat16)
        keep = start + offsets < count
        place = ((cols_now[None, :] == col_ids[:, None]) & keep[None, :]).astype(jnp.bfloat16)
        both_place = jnp.concatenate([place, place], axis=1)
        both_vals = jnp.concatenate([upper, lower], axis=0).reshape(2 * group, 128 * width)
        return accum + jnp.dot(both_place, both_vals, preferred_element_type=jnp.float32)

    accum = jnp.zeros((col_tiles, 128 * width), jnp.float32)
    accum = lax.fori_loop(0, slots // group, add_group, accum)
    partial_value = accum.reshape(col_tiles * 128, width)
    summed = lax.psum_scatter(
        partial_value.astype(jnp.bfloat16), "row", scatter_dimension=0, tiled=True
    )
    grad_features = lax.dot_general(
        summed, weight, (((1,), (1,)), ((), ())), preferred_element_type=jnp.float32
    ).astype(jnp.bfloat16)
    weight_term = lax.dot_general(
        features, summed, (((0,), (0,)), ((), ())), preferred_element_type=jnp.float32
    )
    grad_weight = lax.psum(weight_term, ("row", "col"))
    return (grad_features, grad_weight)


def solution(mesh):
    in_specs = (
        P(("row", "col"), None),
        P(("row", "col"), None),
        P(("col", "row"), None),
        P(),
        P("row", "col", None, None, None),
        P("row", "col", None),
        P("row", "col", None),
        P("row", "col"),
    )
    out_specs = (P(("col", "row"), None), P())
    return jax.shard_map(body, mesh=mesh, in_specs=in_specs, out_specs=out_specs, check_vma=False)
```

profile of v0, /device:TPU:1, one launch (start us, length us, event | category | flops | bytes accessed | tf_op | source)
XLA Modules:
  0.0 803.8 jit_solution(6973166508205975980)
XLA Ops:
  7.2 2.7 compare_select_fusion
  10.1 14.5 %copy.12 = bf16[1,1,320,128,128]{3,4,2,1,0:T(8,128)(2,1)} copy(bf16[1,1,320,128,128]{4,3,2,1,0:T(8,128)(2,1)} %param.14) | data formatting | bytes 20971520 | tf_op args[4]
  24.6 80.9 %all-gather.2.cloned.1.call-done = bf16[16384,256]{1,0:T(8,128)(2,1)} async-done(((bf16[2048,256]{1,0:T(8,128)(2,1)}), bf16[16384,256]{1,0:T(8,128)(2,1)}) %all-gather.2.cloned.1.call-update) | async-done | bytes 8388624 | tf_op jit(solution)/shard_map/all_gather | solution.py:11
  105.4 13.4 %reshape.49 = bf16[128,32768]{1,0:T(8,128)(2,1)} reshape(bf16[16384,256]{1,0:T(8,128)(2,1)} %all-gather.2.cloned.1.call-done) | data formatting | bytes 16777216 | tf_op jit(solution)/shard_map/reshape | solution.py:13
  118.9 342.9 %while.14 = (s32[]{:T(128)}, f32[256,32768]{1,0:T(8,128)}, s32[320]{0:T(512)S(1)}, s32[]{:T(128)}, bf16[320,128,128]{1,2,0:T(8,128)(2,1)}, /*index=5*/s32[320]{0...) while((s32[]{:T(128)}, f32[256,32768]{1,0:T(8,128)}, ...), condition=%wide.region_1.2_spmd.clone, body=%wide.region_0.1_spmd.clone.sunk | while | flops 1634766848 | bytes 110117888 | solution.py:43
  119.8 4.6 convolution_convert_fusion.3
  127.3 2.6 copy.19
  129.8 12.4 %convolution_add_fusion.2 = f32[256,32768]{1,0:T(8,128)} fusion(bf16[64,32768]{1,0:T(8,128)(2,1)S(1)} %bitcast.29, f32[256,32768]{1,0:T(8,128)} %get-tuple-element.281, pred[]{:T(512)S(6)} %compare.3, pred[256,32]{0,1:T(32,128)(4,1)S(1)} %fusion.34), kind=kOutput, calls=%fused_computation.3.clone.1 | convolution fusion | flops 1090535424 | bytes 71311360 | tf_op jit(solution)/shard_map/while/body/eval_jaxpr/dot_general | solution.py:40
  143.2 4.6 convolution_convert_fusion.3
  153.2 24.6 %convolution_add_fusion.2 = f32[256,32768]{1,0:T(8,128)} fusion(bf16[64,32768]{1,0:T(8,128)(2,1)S(1)} %bitcast.29, f32[256,32768]{1,0:T(8,128)} %get-tuple-element.281, pred[]{:T(512)S(6)} %compare.3, pred[256,32]{0,1:T(32,128)(4,1)S(1)} %fusion.34), kind=kOutput, calls=%fused_computation.3.clone.1 | convolution fusion | flops 1090535424 | bytes 71311360 | tf_op jit(solution)/shard_map/while/body/eval_jaxpr/dot_general | solution.py:40
  178.7 4.6 convolution_convert_fusion.3
  186.1 2.6 copy.19
  188.7 24.6 %convolution_add_fusion.2 = f32[256,32768]{1,0:T(8,128)} fusion(bf16[64,32768]{1,0:T(8,128)(2,1)S(1)} %bitcast.29, f32[256,32768]{1,0:T(8,128)} %get-tuple-element.281, pred[]{:T(512)S(6)} %compare.3, pred[256,32]{0,1:T(32,128)(4,1)S(1)} %fusion.34), kind=kOutput, calls=%fused_computation.3.clone.1 | convolution fusion | flops 1090535424 | bytes 71311360 | tf_op jit(solution)/shard_map/while/body/eval_jaxpr/dot_general | solution.py:40
  214.2 4.6 convolution_convert_fusion.3
  224.2 24.6 %convolution_add_fusion.2 = f32[256,32768]{1,0:T(8,128)} fusion(bf16[64,32768]{1,0:T(8,128)(2,1)S(1)} %bitcast.29, f32[256,32768]{1,0:T(8,128)} %get-tuple-element.281, pred[]{:T(512)S(6)} %compare.3, pred[256,32]{0,1:T(32,128)(4,1)S(1)} %fusion.34), kind=kOutput, calls=%fused_computation.3.clone.1 | convolution fusion | flops 1090535424 | bytes 71311360 | tf_op jit(solution)/shard_map/while/body/eval_jaxpr/dot_general | solution.py:40
  249.7 4.6 convolution_convert_fusion.3
  259.7 24.6 %convolution_add_fusion.2 = f32[256,32768]{1,0:T(8,128)} fusion(bf16[64,32768]{1,0:T(8,128)(2,1)S(1)} %bitcast.29, f32[256,32768]{1,0:T(8,128)} %get-tuple-element.281, pred[]{:T(512)S(6)} %compare.3, pred[256,32]{0,1:T(32,128)(4,1)S(1)} %fusion.34), kind=kOutput, calls=%fused_computation.3.clone.1 | convolution fusion | flops 1090535424 | bytes 71311360 | tf_op jit(solution)/shard_map/while/body/eval_jaxpr/dot_general | solution.py:40
  285.2 4.6 convolution_convert_fusion.3
  295.2 24.6 %convolution_add_fusion.2 = f32[256,32768]{1,0:T(8,128)} fusion(bf16[64,32768]{1,0:T(8,128)(2,1)S(1)} %bitcast.29, f32[256,32768]{1,0:T(8,128)} %get-tuple-element.281, pred[]{:T(512)S(6)} %compare.3, pred[256,32]{0,1:T(32,128)(4,1)S(1)} %fusion.34), kind=kOutput, calls=%fused_computation.3.clone.1 | convolution fusion | flops 1090535424 | bytes 71311360 | tf_op jit(solution)/shard_map/while/body/eval_jaxpr/dot_general | solution.py:40
  320.7 4.6 convolution_convert_fusion.3
  330.7 24.6 %convolution_add_fusion.2 = f32[256,32768]{1,0:T(8,128)} fusion(bf16[64,32768]{1,0:T(8,128)(2,1)S(1)} %bitcast.29, f32[256,32768]{1,0:T(8,128)} %get-tuple-element.281, pred[]{:T(512)S(6)} %compare.3, pred[256,32]{0,1:T(32,128)(4,1)S(1)} %fusion.34), kind=kOutput, calls=%fused_computation.3.clone.1 | convolution fusion | flops 1090535424 | bytes 71311360 | tf_op jit(solution)/shard_map/while/body/eval_jaxpr/dot_general | solution.py:40
  356.2 4.6 convolution_convert_fusion.3
  366.2 24.6 %convolution_add_fusion.2 = f32[256,32768]{1,0:T(8,128)} fusion(bf16[64,32768]{1,0:T(8,128)(2,1)S(1)} %bitcast.29, f32[256,32768]{1,0:T(8,128)} %get-tuple-element.281, pred[]{:T(512)S(6)} %compare.3, pred[256,32]{0,1:T(32,128)(4,1)S(1)} %fusion.34), kind=kOutput, calls=%fused_computation.3.clone.1 | convolution fusion | flops 1090535424 | bytes 71311360 | tf_op jit(solution)/shard_map/while/body/eval_jaxpr/dot_general | solution.py:40
  391.7 4.6 convolution_convert_fusion.3
  401.7 24.6 %convolution_add_fusion.2 = f32[256,32768]{1,0:T(8,128)} fusion(bf16[64,32768]{1,0:T(8,128)(2,1)S(1)} %bitcast.29, f32[256,32768]{1,0:T(8,128)} %get-tuple-element.281, pred[]{:T(512)S(6)} %compare.3, pred[256,32]{0,1:T(32,128)(4,1)S(1)} %fusion.34), kind=kOutput, calls=%fused_computation.3.clone.1 | convolution fusion | flops 1090535424 | bytes 71311360 | tf_op jit(solution)/shard_map/while/body/eval_jaxpr/dot_general | solution.py:40
  427.2 4.6 convolution_convert_fusion.3
  437.2 24.6 %convolution_add_fusion.2 = f32[256,32768]{1,0:T(8,128)} fusion(bf16[64,32768]{1,0:T(8,128)(2,1)S(1)} %bitcast.29, f32[256,32768]{1,0:T(8,128)} %get-tuple-element.281, pred[]{:T(512)S(6)} %compare.3, pred[256,32]{0,1:T(32,128)(4,1)S(1)} %fusion.34), kind=kOutput, calls=%fused_computation.3.clone.1 | convolution fusion | flops 1090535424 | bytes 71311360 | tf_op jit(solution)/shard_map/while/body/eval_jaxpr/dot_general | solution.py:40
  461.8 17.1 %convert_element_type.45 = bf16[256,32768]{1,0:T(8,128)(2,1)} convert(f32[256,32768]{1,0:T(8,128)} %get-tuple-element.171) | non-fusion elementwise | flops 8388608 | bytes 50331648 | tf_op jit(solution)/shard_map/convert_element_type | solution.py:46
  478.9 25.6 %convert_element_type.46 = bf16[32768,256]{1,0:T(8,128)(2,1)} reshape(bf16[256,32768]{1,0:T(8,128)(2,1)} %convert_element_type.45) | data formatting | bytes 33554432 | tf_op jit(solution)/shard_map/convert_element_type | solution.py:46
  504.6 145.1 %reduce-scatter.2.cloned.1.call-done = bf16[2048,256]{1,0:T(8,128)(2,1)} async-done(((bf16[32768,256]{1,0:T(8,128)(2,1)}), bf16[2048,256]{1,0:T(8,128)(2,1)}) %reduce-scatter.2.cloned.1.call-update) | async-done | bytes 1048592 | tf_op jit(solution)/shard_map/reduce_scatter | solution.py:45
  652.1 2.7 convolution_convert_fusion.1
  654.8 140.8 %all-reduce.2.cloned.1.call-done = f32[256,256]{0,1:T(8,128)} async-done(((f32[256,256]{0,1:T(8,128)}), f32[256,256]{0,1:T(8,128)}) %all-reduce.2.cloned.1.call-update) | async-done | bytes 262160 | tf_op jit(solution)/shard_map/psum | solution.py:54
  (97 shorter events, 61.7 us)
Async XLA Ops:
  7.2 642.5 %copy-start = (bf16[2048,256]{1,0:T(8,128)(2,1)S(1)}, bf16[2048,256]{1,0:T(8,128)(2,1)}, u32[]{:S(2)}) copy-start(bf16[2048,256]{1,0:T(8,128)(2,1)} %param.12) | copy-start | bytes 3145732
  7.2 2.9 copy-start.2
  7.2 2.9 copy-start.3
  7.2 98.2 %all-gather.2.cloned.1.call-start = ((), (), s32[]{:S(2)}) async-start(), calls=%async_computation.1 | async-start | bytes 9437184 | tf_op jit(solution)/shard_map/all_gather | solution.py:11
  10.0 639.7 %reduce-scatter.2.cloned.1.call-start = ((), (), s32[]{:S(2)}) async-start(), calls=%async_computation.2 | async-start | bytes 17825792 | tf_op jit(solution)/shard_map/reduce_scatter | solution.py:45
  504.5 147.6 %copy-start.1 = (bf16[256,256]{1,0:T(8,128)(2,1)S(1)}, bf16[256,256]{1,0:T(8,128)(2,1)}, u32[]{:S(2)}) copy-start(bf16[256,256]{1,0:T(8,128)(2,1)} %param.13) | copy-start | bytes 393220
  504.6 291.0 %all-reduce.2.cloned.1.call-start = ((), (), s32[]{:S(2)}) async-start(), calls=%async_computation.3 | async-start | bytes 524288 | tf_op jit(solution)/shard_map/psum | solution.py:54
Sparse Core Ops, SparseCore 0:
  10.3 95.1 all-gather.1
  504.7 144.9 reduce-scatter.1
  655.7 139.7 all-reduce.1
where the time goes:
time: 806 us; the launch traced here: 804 us
  waiting for transfers between devices  367 us (46%)
  matrix products  304 us (38%)
  local copies, waits for them, and re-layouts  87.5 us (11%)
  other arithmetic  30.8 us (4%)
  between operations  13.8 us (2%)
    dot_general x10, matrix products, add_group(): jnp.dot(both_place, both_vals, preferred_element_type=jnp.float32)  234 us
    reduce_scatter x1, waiting for transfers between devices, body(): lax.psum_scatter(partial_value.astype(jnp.bfloat16), 'row', scatter_dimen...  145 us
    psum x1, waiting for transfers between devices, body(): grad_weight = lax.psum(weight_term, ('row', 'col'))  141 us
    all_gather x1, waiting for transfers between devices, body(): block = lax.all_gather(masked, 'col', axis=0, tiled=True)  80.9 us
    dot_general x10, matrix products, add_group(): jnp.dot(pick, row_flat, preferred_element_type=jnp.float32)  46.4 us
    while x20, local copies, waits for them, and re-layouts  30.6 us
    convert_element_type x1, local copies, waits for them, and re-layouts, body(): partial_value.astype(jnp.bfloat16)  25.6 us
    dot_general x10, matrix products, add_group(): jnp.einsum('kab,kaf->kbf', tile_blk, gathered, preferred_element_type=jnp...  19.4 us
  transfers between devices with their start and end apart: 3, of which 3 were waited for; matrix products, arithmetic and copies ran while one was open for 2% of the time, Pallas kernels for 0%

commit v1 on v0

--- a/solution.py
+++ b/solution.py
@@ -51,7 +51,7 @@
     weight_term = lax.dot_general(
         features, summed, (((0,), (0,)), ((), ())), preferred_element_type=jnp.float32
     )
-    grad_weight = lax.psum(weight_term, ("row", "col"))
+    grad_weight = jnp.sum(lax.all_gather(weight_term, ("row", "col")), axis=0)
     return (grad_features, grad_weight)
 
 

time: 806 us -> 1030 us (1.28)
  waiting for transfers between devices: 367 us -> 570 us
  local copies, waits for them, and re-layouts: 87.5 us -> 106 us
    all_gather x0 -> x1, waiting for transfers between devices: none -> 345 us  [body(): grad_weight = jnp.sum(lax.all_gather(weight_term, ('row', 'col')), axis=0)]
    psum x1 -> x0, waiting for transfers between devices: 141 us -> none  [body(): grad_weight = lax.psum(weight_term, ('row', 'col'))]
    unnamed x10 -> x7, local copies, waits for them, and re-layouts: 16.3 us -> 34.9 us
where the time goes in v1:
time: 1030 us
  waiting for transfers between devices  570 us (55%)
  matrix products  304 us (30%)
  local copies, waits for them, and re-layouts  106 us (10%)
  other arithmetic  36.3 us (4%)
  between operations  13.8 us (1%)
    all_gather x1, waiting for transfers between devices, body(): grad_weight = jnp.sum(lax.all_gather(weight_term, ('row', 'col')), axis=0)  345 us
    dot_general x10, matrix products, add_group(): jnp.dot(both_place, both_vals, preferred_element_type=jnp.float32)  234 us
    reduce_scatter x1, waiting for transfers between devices, body(): lax.psum_scatter(partial_value.astype(jnp.bfloat16), 'row', scatter_dimen...  145 us
    all_gather x1, waiting for transfers between devices, body(): block = lax.all_gather(masked, 'col', axis=0, tiled=True)  79.6 us
    dot_general x10, matrix products, add_group(): jnp.dot(pick, row_flat, preferred_element_type=jnp.float32)  46.4 us
    unnamed x7, local copies, waits for them, and re-layouts  34.9 us
    while x20, local copies, waits for them, and re-layouts  30.6 us
    convert_element_type x1, local copies, waits for them, and re-layouts, body(): partial_value.astype(jnp.bfloat16)  25.6 us
  transfers between devices with their start and end apart: 3, of which 3 were waited for; matrix products, arithmetic and copies ran while one was open for 2% of the time, Pallas kernels for 0%

profile of v1, /device:TPU:1, one launch (start us, length us, event | category | flops | bytes accessed | tf_op | source)
XLA Modules:
  0.0 1030.8 jit_solution(17158811552285771586)
XLA Ops:
  7.2 2.7 compare_select_fusion
  11.4 14.4 %copy.13 = bf16[1,1,320,128,128]{3,4,2,1,0:T(8,128)(2,1)} copy(bf16[1,1,320,128,128]{4,3,2,1,0:T(8,128)(2,1)} %param.14) | data formatting | bytes 20971520 | tf_op args[4]
  25.8 79.6 %all-gather.4.cloned.1.call-done = bf16[16384,256]{1,0:T(8,128)(2,1)} async-done(((bf16[2048,256]{1,0:T(8,128)(2,1)}), bf16[16384,256]{1,0:T(8,128)(2,1)}) %all-gather.4.cloned.1.call-update) | async-done | bytes 8388624 | tf_op jit(solution)/shard_map/all_gather | solution.py:11
  105.4 13.4 %reshape.49 = bf16[128,32768]{1,0:T(8,128)(2,1)} reshape(bf16[16384,256]{1,0:T(8,128)(2,1)} %all-gather.4.cloned.1.call-done) | data formatting | bytes 16777216 | tf_op jit(solution)/shard_map/reshape | solution.py:13
  118.9 342.9 %while.14 = (s32[]{:T(128)}, f32[256,32768]{1,0:T(8,128)}, s32[320]{0:T(512)S(1)}, s32[]{:T(128)}, bf16[320,128,128]{1,2,0:T(8,128)(2,1)}, /*index=5*/s32[320]{0...) while((s32[]{:T(128)}, f32[256,32768]{1,0:T(8,128)}, ...), condition=%wide.region_1.2_spmd.clone, body=%wide.region_0.1_spmd.clone.sunk | while | flops 1634766848 | bytes 110117888 | solution.py:43
  119.8 4.6 convolution_convert_fusion.3
  129.8 12.4 %convolution_add_fusion.2 = f32[256,32768]{1,0:T(8,128)} fusion(bf16[64,32768]{1,0:T(8,128)(2,1)S(1)} %bitcast.34, f32[256,32768]{1,0:T(8,128)} %get-tuple-element.281, pred[]{:T(512)S(6)} %compare.3, pred[256,32]{0,1:T(32,128)(4,1)S(1)} %fusion.34), kind=kOutput, calls=%fused_computation.3.clone.1 | convolution fusion | flops 1090535424 | bytes 71311360 | tf_op jit(solution)/shard_map/while/body/eval_jaxpr/dot_general | solution.py:40
  143.1 4.6 convolution_convert_fusion.3
  153.1 24.6 %convolution_add_fusion.2 = f32[256,32768]{1,0:T(8,128)} fusion(bf16[64,32768]{1,0:T(8,128)(2,1)S(1)} %bitcast.34, f32[256,32768]{1,0:T(8,128)} %get-tuple-element.281, pred[]{:T(512)S(6)} %compare.3, pred[256,32]{0,1:T(32,128)(4,1)S(1)} %fusion.34), kind=kOutput, calls=%fused_computation.3.clone.1 | convolution fusion | flops 1090535424 | bytes 71311360 | tf_op jit(solution)/shard_map/while/body/eval_jaxpr/dot_general | solution.py:40
  178.6 4.6 convolution_convert_fusion.3
  188.6 24.6 %convolution_add_fusion.2 = f32[256,32768]{1,0:T(8,128)} fusion(bf16[64,32768]{1,0:T(8,128)(2,1)S(1)} %bitcast.34, f32[256,32768]{1,0:T(8,128)} %get-tuple-element.281, pred[]{:T(512)S(6)} %compare.3, pred[256,32]{0,1:T(32,128)(4,1)S(1)} %fusion.34), kind=kOutput, calls=%fused_computation.3.clone.1 | convolution fusion | flops 1090535424 | bytes 71311360 | tf_op jit(solution)/shard_map/while/body/eval_jaxpr/dot_general | solution.py:40
  214.1 4.6 convolution_convert_fusion.3
  224.1 24.6 %convolution_add_fusion.2 = f32[256,32768]{1,0:T(8,128)} fusion(bf16[64,32768]{1,0:T(8,128)(2,1)S(1)} %bitcast.34, f32[256,32768]{1,0:T(8,128)} %get-tuple-element.281, pred[]{:T(512)S(6)} %compare.3, pred[256,32]{0,1:T(32,128)(4,1)S(1)} %fusion.34), kind=kOutput, calls=%fused_computation.3.clone.1 | convolution fusion | flops 1090535424 | bytes 71311360 | tf_op jit(solution)/shard_map/while/body/eval_jaxpr/dot_general | solution.py:40
  249.6 4.6 convolution_convert_fusion.3
  259.6 24.6 %convolution_add_fusion.2 = f32[256,32768]{1,0:T(8,128)} fusion(bf16[64,32768]{1,0:T(8,128)(2,1)S(1)} %bitcast.34, f32[256,32768]{1,0:T(8,128)} %get-tuple-element.281, pred[]{:T(512)S(6)} %compare.3, pred[256,32]{0,1:T(32,128)(4,1)S(1)} %fusion.34), kind=kOutput, calls=%fused_computation.3.clone.1 | convolution fusion | flops 1090535424 | bytes 71311360 | tf_op jit(solution)/shard_map/while/body/eval_jaxpr/dot_general | solution.py:40
  285.1 4.6 convolution_convert_fusion.3
  295.1 24.6 %convolution_add_fusion.2 = f32[256,32768]{1,0:T(8,128)} fusion(bf16[64,32768]{1,0:T(8,128)(2,1)S(1)} %bitcast.34, f32[256,32768]{1,0:T(8,128)} %get-tuple-element.281, pred[]{:T(512)S(6)} %compare.3, pred[256,32]{0,1:T(32,128)(4,1)S(1)} %fusion.34), kind=kOutput, calls=%fused_computation.3.clone.1 | convolution fusion | flops 1090535424 | bytes 71311360 | tf_op jit(solution)/shard_map/while/body/eval_jaxpr/dot_general | solution.py:40
  320.6 4.6 convolution_convert_fusion.3
  330.6 24.6 %convolution_add_fusion.2 = f32[256,32768]{1,0:T(8,128)} fusion(bf16[64,32768]{1,0:T(8,128)(2,1)S(1)} %bitcast.34, f32[256,32768]{1,0:T(8,128)} %get-tuple-element.281, pred[]{:T(512)S(6)} %compare.3, pred[256,32]{0,1:T(32,128)(4,1)S(1)} %fusion.34), kind=kOutput, calls=%fused_computation.3.clone.1 | convolution fusion | flops 1090535424 | bytes 71311360 | tf_op jit(solution)/shard_map/while/body/eval_jaxpr/dot_general | solution.py:40
  356.1 4.6 convolution_convert_fusion.3
  366.1 24.6 %convolution_add_fusion.2 = f32[256,32768]{1,0:T(8,128)} fusion(bf16[64,32768]{1,0:T(8,128)(2,1)S(1)} %bitcast.34, f32[256,32768]{1,0:T(8,128)} %get-tuple-element.281, pred[]{:T(512)S(6)} %compare.3, pred[256,32]{0,1:T(32,128)(4,1)S(1)} %fusion.34), kind=kOutput, calls=%fused_computation.3.clone.1 | convolution fusion | flops 1090535424 | bytes 71311360 | tf_op jit(solution)/shard_map/while/body/eval_jaxpr/dot_general | solution.py:40
  391.6 4.6 convolution_convert_fusion.3
  401.6 24.6 %convolution_add_fusion.2 = f32[256,32768]{1,0:T(8,128)} fusion(bf16[64,32768]{1,0:T(8,128)(2,1)S(1)} %bitcast.34, f32[256,32768]{1,0:T(8,128)} %get-tuple-element.281, pred[]{:T(512)S(6)} %compare.3, pred[256,32]{0,1:T(32,128)(4,1)S(1)} %fusion.34), kind=kOutput, calls=%fused_computation.3.clone.1 | convolution fusion | flops 1090535424 | bytes 71311360 | tf_op jit(solution)/shard_map/while/body/eval_jaxpr/dot_general | solution.py:40
  427.1 4.6 convolution_convert_fusion.3
  437.1 24.6 %convolution_add_fusion.2 = f32[256,32768]{1,0:T(8,128)} fusion(bf16[64,32768]{1,0:T(8,128)(2,1)S(1)} %bitcast.34, f32[256,32768]{1,0:T(8,128)} %get-tuple-element.281, pred[]{:T(512)S(6)} %compare.3, pred[256,32]{0,1:T(32,128)(4,1)S(1)} %fusion.34), kind=kOutput, calls=%fused_computation.3.clone.1 | convolution fusion | flops 1090535424 | bytes 71311360 | tf_op jit(solution)/shard_map/while/body/eval_jaxpr/dot_general | solution.py:40
  461.7 17.1 %convert_element_type.45 = bf16[256,32768]{1,0:T(8,128)(2,1)} convert(f32[256,32768]{1,0:T(8,128)} %get-tuple-element.171) | non-fusion elementwise | flops 8388608 | bytes 50331648 | tf_op jit(solution)/shard_map/convert_element_type | solution.py:46
  478.8 25.6 %convert_element_type.46 = bf16[32768,256]{1,0:T(8,128)(2,1)} reshape(bf16[256,32768]{1,0:T(8,128)(2,1)} %convert_element_type.45) | data formatting | bytes 33554432 | tf_op jit(solution)/shard_map/convert_element_type | solution.py:46
  504.7 145.2 %reduce-scatter.2.cloned.1.call-done = bf16[2048,256]{1,0:T(8,128)(2,1)} async-done(((bf16[32768,256]{1,0:T(8,128)(2,1)}), bf16[2048,256]{1,0:T(8,128)(2,1)}) %reduce-scatter.2.cloned.1.call-update) | async-done | bytes 1048592 | tf_op jit(solution)/shard_map/reduce_scatter | solution.py:45
  652.3 2.7 convolution_convert_fusion.1
  655.0 344.7 %all-gather.6.cloned.1.call-done = f32[32768,256]{0,1:T(8,128)} async-done(((f32[256,256]{0,1:T(8,128)}), f32[32768,256]{0,1:T(8,128)}) %all-gather.6.cloned.1.call-update) | async-done | bytes 33554448 | tf_op jit(solution)/shard_map/all_gather | solution.py:54
  999.7 19.6 %copy.17 = f32[32,8,128,256]{3,2,1,0:T(8,128)S(1)} copy(f32[32,8,128,256]{3,1,2,0:T(8,128)} %bitcast.38) | data formatting | bytes 67108864
  1019.3 4.1 bitcast_reduce_fusion
  (95 shorter events, 67.4 us)
Async XLA Ops:
  7.2 642.7 %copy-start = (bf16[2048,256]{1,0:T(8,128)(2,1)S(1)}, bf16[2048,256]{1,0:T(8,128)(2,1)}, u32[]{:S(2)}) copy-start(bf16[2048,256]{1,0:T(8,128)(2,1)} %param.12) | copy-start | bytes 3145732
  7.2 98.2 %all-gather.4.cloned.1.call-start = ((), (), s32[]{:S(2)}) async-start(), calls=%async_computation.1 | async-start | bytes 9437184 | tf_op jit(solution)/shard_map/all_gather | solution.py:11
  10.0 639.9 %reduce-scatter.2.cloned.1.call-start = ((), (), s32[]{:S(2)}) async-start(), calls=%async_computation.2 | async-start | bytes 17825792 | tf_op jit(solution)/shard_map/reduce_scatter | solution.py:45
  504.5 147.8 %copy-start.1 = (bf16[256,256]{1,0:T(8,128)(2,1)S(1)}, bf16[256,256]{1,0:T(8,128)(2,1)}, u32[]{:S(2)}) copy-start(bf16[256,256]{1,0:T(8,128)(2,1)} %param.13) | copy-start | bytes 393220
  504.5 495.2 %all-gather.6.cloned.1.call-start = ((), (), s32[]{:S(2)}) async-start(), calls=%async_computation.3 | async-start | bytes 33816576 | tf_op jit(solution)/shard_map/all_gather | solution.py:54
Sparse Core Ops, SparseCore 0:
  10.2 95.1 all-gather.3
  504.6 145.2 reduce-scatter.1
  652.4 347.2 all-gather.5
